TPU v7x, 32 devices: a whole 2x2x4 slice. The times are simulated.
32 devices in a mesh: tm: 8 (over y, x, core), space: 4 (over z).
Axes of the slice: x: 2, y: 2, z: 4, core: 2. Of those that a mesh axis runs over, the one named last changes fastest.
Arguments:
- states_old: float32 [8, 41, 32768], P('tm', None, 'space'), may hold values from -6 to 6
- coupling: float32 [256, 2, 128, 128], P('space'), may hold values from 0 to 0.1
- gate_center: float32 [40, 1], replicated, may hold values from -1 to 1
- gate_slope: float32 [40, 1], replicated, may hold values from 0.3 to 1
- gate_rate: float32 [40, 1], replicated, may hold values from 0.02 to 2
- reversal: float32 [40, 1], replicated, may hold values from -2 to 2
- conductance: float32 [40, 32768], P(None, 'space'), may hold values from 0.001 to 0.03
- stimulus: float32 [8, 32768], P('tm', 'space'), may hold values from -3 to 3
- coarse_rate: float32 [41, 32768], P(None, 'space'), may hold values from 0.025 to 1.25
Outputs:
- states_new: float32 [8, 41, 32768], P('tm', None, 'space')
- voltage_new: float32 [8, 32768], P('tm', 'space')
All inputs are finite; a program needn't handle non-finite values.
Results may differ from a plain program's by a relative error of at most 0.0003.
Values sent between devices are 32-bit elements; how exact they have to be, the bound alone decides.
No kernel may reach another device: no remote copies, remote signals or barrier semaphores. Data moves between devices by JAX's collectives and lax.ppermute only.
A program may use at most 192 MiB of HBM per device.

v0:
```python
import jax
import jax.numpy as jnp
from jax import lax
from jax.sharding import PartitionSpec as P

FINE = 2
SUB = 2
CG_ITERS = 8


HIGHEST_PRECISION = lax.Precision.HIGHEST


def passed_along(value, axis, steps):
    count = lax.axis_size(axis)
    leading, last = (max(0, -steps), min(count, count - steps))
    return lax.ppermute(value, axis, [(source, source + steps) for source in range(leading, last)])


def entering(shard, axis, combine, identity):
    peers, mine = (lax.axis_size(axis), lax.axis_index(axis))
    everything = jax.tree.map(lambda part: lax.all_gather(part, axis), shard)
    start = jax.tree.map(
        lambda part, zero: jnp.broadcast_to(jnp.asarray(zero, part.dtype), part.shape),
        shard,
        identity,
    )

    def hop(k, before):
        reached = k < mine
        new = combine(before, jax.tree.map(lambda part: part[k], everything))
        return jax.tree.map(lambda a, b: jnp.where(reached, a, b), new, before)

    return lax.fori_loop(0, peers, hop, start)


def broadcast(shard, axis, root):
    mine = lax.axis_index(axis) == root
    return lax.psum(jnp.where(mine, shard, jnp.zeros_like(shard)), axis)


def ionic_update(voltage, gating, conductance, gate_center, gate_slope, gate_rate, reversal):
    for substep in range(SUB):
        steady = jax.nn.sigmoid((voltage[None, :] - gate_center) / gate_slope)
        damping = jnp.exp(-gate_rate * (0.5 + steady))
        gating = steady + (gating - steady) * damping
        current = jnp.sum(conductance * gating * (voltage[None, :] - reversal), axis=0)
        voltage = voltage - current
    return (voltage, gating)


def matvec_rows(tiles, values):
    return jnp.einsum("bik,bk->bi", tiles, values, precision=HIGHEST_PRECISION)


def compose_pair(earlier, later):
    return (later[0] * earlier[0], later[0] * earlier[1] + later[1])


def body(
    states_old,
    coupling,
    gate_center,
    gate_slope,
    gate_rate,
    reversal,
    conductance,
    stimulus,
    coarse_rate,
):
    num_blocks = coupling.shape[0]
    tile_width = coupling.shape[2]
    zero_rows = jnp.zeros((2, tile_width), jnp.float32)

    def couple(vector):
        upper_rows = passed_along(vector[:2], "space", -1)
        extended = jnp.concatenate([vector, upper_rows], axis=0)
        ahead_sum = matvec_rows(coupling[:, 0], extended[1 : num_blocks + 1]) + matvec_rows(
            coupling[:, 1], extended[2 : num_blocks + 2]
        )
        carried = jnp.einsum("bjki,bk->bji", coupling, vector, precision=HIGHEST_PRECISION)
        inner = jnp.concatenate([zero_rows[:1], carried[:-1, 0]], axis=0) + jnp.concatenate(
            [zero_rows, carried[:-2, 1]], axis=0
        )
        spilled = jnp.stack([carried[-1, 0] + carried[-2, 1], carried[-1, 1]])
        arrived = passed_along(spilled, "space", 1)
        behind = inner + jnp.concatenate(
            [arrived, jnp.zeros((num_blocks - 2, tile_width), jnp.float32)], axis=0
        )
        return ahead_sum + behind

    degree = couple(jnp.ones((num_blocks, tile_width), jnp.float32))

    def operate(vector):
        return vector + degree * vector - couple(vector)

    def squares(vector):
        return lax.psum(jnp.sum(vector * vector), "space")

    voltage = states_old[0, 0]
    gating = states_old[0, 1:]
    for fine_step in range(FINE):
        voltage, gating = ionic_update(
            voltage, gating, conductance, gate_center, gate_slope, gate_rate, reversal
        )
        voltage = voltage + stimulus[0]
        right_side = voltage.reshape(num_blocks, tile_width)
        iterate = right_side
        residual = right_side - operate(right_side)
        direction = residual
        norm_now = squares(residual)
        for iteration in range(CG_ITERS):
            mapped = operate(direction)
            step_size = norm_now / lax.psum(jnp.sum(direction * mapped), "space")
            iterate = iterate + step_size * direction
            residual = residual - step_size * mapped
            norm_next = squares(residual)
            direction = residual + norm_next / norm_now * direction
            norm_now = norm_next
        voltage = iterate.reshape(-1)
    fine_state = jnp.concatenate([voltage[None, :], gating], axis=0)
    factor = jnp.exp(-coarse_rate * (1.0 + jax.nn.sigmoid(states_old[0, 0]))[None, :])
    offset = fine_state - factor * states_old[0]
    identity = (jnp.ones_like(factor), jnp.zeros_like(offset))
    prefix = entering((factor, offset), "tm", compose_pair, identity)
    through = compose_pair(prefix, (factor, offset))
    last_slice = lax.axis_size("tm") - 1
    total_map = broadcast(jnp.stack([through[0], through[1]]), "tm", last_slice)
    start_state = total_map[1] / (1.0 - total_map[0])
    new_state = prefix[0] * start_state + prefix[1]
    return (new_state[None], new_state[0][None])


def solution(mesh):
    return jax.shard_map(
        body,
        mesh=mesh,
        in_specs=(
            P("tm", None, "space"),
            P("space", None, None, None),
            P(),
            P(),
            P(),
            P(),
            P(None, "space"),
            P("tm", "space"),
            P(None, "space"),
        ),
        out_specs=(P("tm", None, "space"), P("tm", "space")),
        check_vma=False,
    )
```

profile of v0, /device:TPU:0, one launch (start us, length us, event | category | flops | bytes accessed | tf_op | source)
XLA Modules:
  0.0 1167.4 jit_solution(7216725243608075345)
XLA Ops:
  86.8 10.6 all-reduce.59
  99.4 9.8 psum.233
  140.2 10.3 psum.234
  193.3 10.2 psum.236
  246.4 10.2 psum.238
  299.7 10.2 psum.240
  352.8 10.1 psum.242
  364.8 9.8 psum.243
  405.9 10.1 psum.244
  417.9 9.9 psum.245
  459.1 10.0 psum.246
  523.4 9.9 all-reduce.58
  535.1 10.5 psum.249
  576.6 9.8 psum.250
  588.4 10.1 psum.251
  641.2 10.2 psum.253
  694.2 10.2 psum.255
  747.1 10.2 psum.257
  800.4 10.3 psum.259
  853.2 10.3 psum.261
  911.1 70.5 %all-gather.7.cloned.1.call-done = f32[8,41,8192]{2,1,0:T(8,128)} async-done(((f32[1,41,8192]{2,1,0:T(8,128)}), f32[8,41,8192]{2,1,0:T(8,128)}) %all-gather.7.cloned.1.call-update) | async-done | bytes 10747920 | tf_op jit(solution)/shard_map/all_gather | solution.py:22
  981.6 74.0 %all-gather.9.cloned.1.call-done = f32[8,41,8192]{2,1,0:T(8,128)} async-done(((f32[1,41,8192]{2,1,0:T(8,128)}), f32[8,41,8192]{2,1,0:T(8,128)}) %all-gather.9.cloned.1.call-update) | async-done | bytes 10747920 | tf_op jit(solution)/shard_map/all_gather | solution.py:22
  1055.6 24.7 %while.16 = (s32[]{:T(128)}, f32[41,8192]{1,0:T(8,128)S(1)}, f32[41,8192]{1,0:T(8,128)S(1)}, s32[]{:T(128)}, f32[8,41,8192]{2,1,0:T(8,128)}, /*index=5*/f32[8,41,8192]{2,1,0:T(8,128)}, s32[]{:T(128)}, s32[]{:T(128)}) while((s32[]{:T(128)}, f32[41,8192]{1,0:T(8,128)S(1)}, f32[41,8192]{1,0:T(8,128)S(1)}, s32[]{:T(128)}, ...), condition=%wide.region_69.70_spmd.clone, body=%wide.region_68.69_spmd.clone.sunk | while | flops 2351108 | bytes 8061037 | solution.py:34
  1085.8 69.6 %all-reduce.62.cloned.1.call-done = f32[2,41,8192]{2,1,0:T(8,128)} async-done(((f32[2,41,8192]{2,1,0:T(8,128)}), f32[2,41,8192]{2,1,0:T(8,128)}) %all-reduce.62.cloned.1.call-update) | async-done | bytes 2686992 | tf_op jit(solution)/shard_map/psum | solution.py:39
  (377 shorter events, 695.7 us)
Async XLA Ops:
  7.2 974.4 %all-gather.7.cloned.1.call-start = ((), (), s32[]{:S(2)}) async-start(), calls=%async_computation.1 | async-start | bytes 14155776 | tf_op jit(solution)/shard_map/all_gather | solution.py:22
  18.8 43.1 %collective-permute-start.3 = (f32[2,128]{1,0:T(2,128)S(1)}, f32[2,128]{1,0:T(2,128)S(1)}, u32[]{:S(2)}, u32[]{:S(2)}) collective-permute-start(f32[2,128]{1,0:T(2,128)S(1)} %pad_maximum_fusion.19), channel_id=1, source_target_pairs={{0,1},{1,2},{2,3},{4,5},{5,6},{6,7},{8,9},{9,10},{10,11},{12,13},{... | collective-permute-start | bytes 3080 | tf_op jit(solution)/shard_map/ppermute | solution.py:17
  23.8 11.5 collective-permute-start.2
  29.2 32.7 %collective-permute-start.1 = (f32[2,128]{1,0:T(2,128)S(1)}, f32[2,128]{1,0:T(2,128)S(1)}, u32[]{:S(2)}, u32[]{:S(2)}) collective-permute-start(f32[2,128]{1,0:T(2,128)S(1)} %pad_maximum_fusion.18), channel_id=1, source_target_pairs={{0,1},{1,2},{2,3},{4,5},{5,6},{6,7},{8,9},{9,10},{10,11},{12,13},{... | collective-permute-start | bytes 3080 | tf_op jit(solution)/shard_map/ppermute | solution.py:17
  33.7 14.7 %collective-permute-start = (f32[2,128]{1,0:T(2,128)S(1)}, f32[2,128]{1,0:T(2,128)S(1)}, u32[]{:S(2)}, u32[]{:S(2)}) collective-permute-start(f32[2,128]{1,0:T(2,128)S(1)} %slice.520), channel_id=1, source_target_pairs={{1,0},{2,1},{3,2},{5,4},{6,5},{7,6},{9,8},{10,9},{11,10},{13,12},{... | collective-permute-start | bytes 3080 | tf_op jit(solution)/shard_map/ppermute | solution.py:17
  67.8 18.4 %collective-permute-start.5 = (f32[2,128]{1,0:T(2,128)S(1)}, f32[2,128]{1,0:T(2,128)S(1)}, u32[]{:S(2)}, u32[]{:S(2)}) collective-permute-start(f32[2,128]{1,0:T(2,128)S(1)} %pad_maximum_fusion.20), channel_id=1, source_target_pairs={{0,1},{1,2},{2,3},{4,5},{5,6},{6,7},{8,9},{9,10},{10,11},{12,13},{... | collective-permute-start | bytes 3080 | tf_op jit(solution)/shard_map/ppermute | solution.py:17
  118.3 21.2 %collective-permute-start.7 = (f32[2,128]{1,0:T(2,128)S(1)}, f32[2,128]{1,0:T(2,128)S(1)}, u32[]{:S(2)}, u32[]{:S(2)}) collective-permute-start(f32[2,128]{1,0:T(2,128)S(1)} %pad_maximum_fusion.21), channel_id=1, source_target_pairs={{0,1},{1,2},{2,3},{4,5},{5,6},{6,7},{8,9},{9,10},{10,11},{12,13},{... | collective-permute-start | bytes 3080 | tf_op jit(solution)/shard_map/ppermute | solution.py:17
  171.2 21.4 %collective-permute-start.9 = (f32[2,128]{1,0:T(2,128)S(1)}, f32[2,128]{1,0:T(2,128)S(1)}, u32[]{:S(2)}, u32[]{:S(2)}) collective-permute-start(f32[2,128]{1,0:T(2,128)S(1)} %pad_maximum_fusion.22), channel_id=1, source_target_pairs={{0,1},{1,2},{2,3},{4,5},{5,6},{6,7},{8,9},{9,10},{10,11},{12,13},{... | collective-permute-start | bytes 3080 | tf_op jit(solution)/shard_map/ppermute | solution.py:17
  224.3 21.5 %collective-permute-start.11 = (f32[2,128]{1,0:T(2,128)S(1)}, f32[2,128]{1,0:T(2,128)S(1)}, u32[]{:S(2)}, u32[]{:S(2)}) collective-permute-start(f32[2,128]{1,0:T(2,128)S(1)} %pad_maximum_fusion.23), channel_id=1, source_target_pairs={{0,1},{1,2},{2,3},{4,5},{5,6},{6,7},{8,9},{9,10},{10,11},{12,13},{... | collective-permute-start | bytes 3080 | tf_op jit(solution)/shard_map/ppermute | solution.py:17
  277.4 21.7 %collective-permute-start.13 = (f32[2,128]{1,0:T(2,128)S(1)}, f32[2,128]{1,0:T(2,128)S(1)}, u32[]{:S(2)}, u32[]{:S(2)}) collective-permute-start(f32[2,128]{1,0:T(2,128)S(1)} %pad_maximum_fusion.24), channel_id=1, source_target_pairs={{0,1},{1,2},{2,3},{4,5},{5,6},{6,7},{8,9},{9,10},{10,11},{12,13},{... | collective-permute-start | bytes 3080 | tf_op jit(solution)/shard_map/ppermute | solution.py:17
  330.7 21.4 %collective-permute-start.15 = (f32[2,128]{1,0:T(2,128)S(1)}, f32[2,128]{1,0:T(2,128)S(1)}, u32[]{:S(2)}, u32[]{:S(2)}) collective-permute-start(f32[2,128]{1,0:T(2,128)S(1)} %pad_maximum_fusion.25), channel_id=1, source_target_pairs={{0,1},{1,2},{2,3},{4,5},{5,6},{6,7},{8,9},{9,10},{10,11},{12,13},{... | collective-permute-start | bytes 3080 | tf_op jit(solution)/shard_map/ppermute | solution.py:17
  383.8 21.4 %collective-permute-start.17 = (f32[2,128]{1,0:T(2,128)S(1)}, f32[2,128]{1,0:T(2,128)S(1)}, u32[]{:S(2)}, u32[]{:S(2)}) collective-permute-start(f32[2,128]{1,0:T(2,128)S(1)} %pad_maximum_fusion.26), channel_id=1, source_target_pairs={{0,1},{1,2},{2,3},{4,5},{5,6},{6,7},{8,9},{9,10},{10,11},{12,13},{... | collective-permute-start | bytes 3080 | tf_op jit(solution)/shard_map/ppermute | solution.py:17
  436.9 21.6 %collective-permute-start.19 = (f32[2,128]{1,0:T(2,128)S(1)}, f32[2,128]{1,0:T(2,128)S(1)}, u32[]{:S(2)}, u32[]{:S(2)}) collective-permute-start(f32[2,128]{1,0:T(2,128)S(1)} %pad_maximum_fusion.27), channel_id=1, source_target_pairs={{0,1},{1,2},{2,3},{4,5},{5,6},{6,7},{8,9},{9,10},{10,11},{12,13},{... | collective-permute-start | bytes 3080 | tf_op jit(solution)/shard_map/ppermute | solution.py:17
  481.2 18.0 %collective-permute-start.21 = (f32[2,128]{1,0:T(2,128)S(1)}, f32[2,128]{1,0:T(2,128)S(1)}, u32[]{:S(2)}, u32[]{:S(2)}) collective-permute-start(f32[2,128]{1,0:T(2,128)S(1)} %pad_maximum_fusion.28), channel_id=1, source_target_pairs={{0,1},{1,2},{2,3},{4,5},{5,6},{6,7},{8,9},{9,10},{10,11},{12,13},{... | collective-permute-start | bytes 3080 | tf_op jit(solution)/shard_map/ppermute | solution.py:17
  504.9 17.8 %collective-permute-start.23 = (f32[2,128]{1,0:T(2,128)S(1)}, f32[2,128]{1,0:T(2,128)S(1)}, u32[]{:S(2)}, u32[]{:S(2)}) collective-permute-start(f32[2,128]{1,0:T(2,128)S(1)} %pad_maximum_fusion.29), channel_id=1, source_target_pairs={{0,1},{1,2},{2,3},{4,5},{5,6},{6,7},{8,9},{9,10},{10,11},{12,13},{... | collective-permute-start | bytes 3080 | tf_op jit(solution)/shard_map/ppermute | solution.py:17
  554.7 21.2 %collective-permute-start.25 = (f32[2,128]{1,0:T(2,128)S(1)}, f32[2,128]{1,0:T(2,128)S(1)}, u32[]{:S(2)}, u32[]{:S(2)}) collective-permute-start(f32[2,128]{1,0:T(2,128)S(1)} %pad_maximum_fusion.30), channel_id=1, source_target_pairs={{0,1},{1,2},{2,3},{4,5},{5,6},{6,7},{8,9},{9,10},{10,11},{12,13},{... | collective-permute-start | bytes 3080 | tf_op jit(solution)/shard_map/ppermute | solution.py:17
  607.5 21.4 %collective-permute-start.27 = (f32[2,128]{1,0:T(2,128)S(1)}, f32[2,128]{1,0:T(2,128)S(1)}, u32[]{:S(2)}, u32[]{:S(2)}) collective-permute-start(f32[2,128]{1,0:T(2,128)S(1)} %pad_maximum_fusion.31), channel_id=1, source_target_pairs={{0,1},{1,2},{2,3},{4,5},{5,6},{6,7},{8,9},{9,10},{10,11},{12,13},{... | collective-permute-start | bytes 3080 | tf_op jit(solution)/shard_map/ppermute | solution.py:17
  660.4 21.4 %collective-permute-start.29 = (f32[2,128]{1,0:T(2,128)S(1)}, f32[2,128]{1,0:T(2,128)S(1)}, u32[]{:S(2)}, u32[]{:S(2)}) collective-permute-start(f32[2,128]{1,0:T(2,128)S(1)} %pad_maximum_fusion.32), channel_id=1, source_target_pairs={{0,1},{1,2},{2,3},{4,5},{5,6},{6,7},{8,9},{9,10},{10,11},{12,13},{... | collective-permute-start | bytes 3080 | tf_op jit(solution)/shard_map/ppermute | solution.py:17
  713.4 21.5 %collective-permute-start.31 = (f32[2,128]{1,0:T(2,128)S(1)}, f32[2,128]{1,0:T(2,128)S(1)}, u32[]{:S(2)}, u32[]{:S(2)}) collective-permute-start(f32[2,128]{1,0:T(2,128)S(1)} %pad_maximum_fusion.33), channel_id=1, source_target_pairs={{0,1},{1,2},{2,3},{4,5},{5,6},{6,7},{8,9},{9,10},{10,11},{12,13},{... | collective-permute-start | bytes 3080 | tf_op jit(solution)/shard_map/ppermute | solution.py:17
  766.4 21.7 %collective-permute-start.33 = (f32[2,128]{1,0:T(2,128)S(1)}, f32[2,128]{1,0:T(2,128)S(1)}, u32[]{:S(2)}, u32[]{:S(2)}) collective-permute-start(f32[2,128]{1,0:T(2,128)S(1)} %pad_maximum_fusion.34), channel_id=1, source_target_pairs={{0,1},{1,2},{2,3},{4,5},{5,6},{6,7},{8,9},{9,10},{10,11},{12,13},{... | collective-permute-start | bytes 3080 | tf_op jit(solution)/shard_map/ppermute | solution.py:17
  819.7 21.4 %collective-permute-start.35 = (f32[2,128]{1,0:T(2,128)S(1)}, f32[2,128]{1,0:T(2,128)S(1)}, u32[]{:S(2)}, u32[]{:S(2)}) collective-permute-start(f32[2,128]{1,0:T(2,128)S(1)} %pad_maximum_fusion.35), channel_id=1, source_target_pairs={{0,1},{1,2},{2,3},{4,5},{5,6},{6,7},{8,9},{9,10},{10,11},{12,13},{... | collective-permute-start | bytes 3080 | tf_op jit(solution)/shard_map/ppermute | solution.py:17
  872.6 21.6 %collective-permute-start.37 = (f32[2,128]{1,0:T(2,128)S(1)}, f32[2,128]{1,0:T(2,128)S(1)}, u32[]{:S(2)}, u32[]{:S(2)}) collective-permute-start(f32[2,128]{1,0:T(2,128)S(1)} %pad_maximum_fusion.36), channel_id=1, source_target_pairs={{0,1},{1,2},{2,3},{4,5},{5,6},{6,7},{8,9},{9,10},{10,11},{12,13},{... | collective-permute-start | bytes 3080 | tf_op jit(solution)/shard_map/ppermute | solution.py:17
  910.3 145.4 %all-gather.9.cloned.1.call-start = ((), (), s32[]{:S(2)}) async-start(), calls=%async_computation.2 | async-start | bytes 14155776 | tf_op jit(solution)/shard_map/all_gather | solution.py:22
  911.0 244.4 %all-reduce.62.cloned.1.call-start = ((), (), s32[]{:S(2)}) async-start(), calls=%async_computation | async-start | bytes 6291456 | tf_op jit(solution)/shard_map/psum | solution.py:39
  (27 other events, 632.6 us)
Sparse Core Ops, SparseCore 0:
  910.4 71.1 all-gather.6
  983.5 72.1 all-gather.8
  1086.0 69.4 all-reduce.61
where the time goes:
time: 1180 us; the launch traced here: 1170 us
  matrix products  412 us (35%)
  blocking collectives  300 us (25%)
  waiting for transfers between devices  215 us (18%)
  starting transfers between devices  116 us (10%)
  other arithmetic  63.3 us (5%)
  between operations  54.8 us (5%)
    dot_general x38, matrix products, matvec_rows(): return jnp.einsum('bik,bk->bi', tiles, values, precision=HIGHEST_PRECISION)  299 us
    psum x16, blocking collectives, squares(): return lax.psum(jnp.sum(vector * vector), 'space')  161 us
    all_gather x2, waiting for transfers between devices, entering(): everything = jax.tree.map(lambda part: lax.all_gather(part, axis), shard)  145 us
    psum x14, blocking collectives, body(): step_size = norm_now / lax.psum(jnp.sum(direction * mapped), 'space')  139 us
    ppermute x38, starting transfers between devices, passed_along(): lax.ppermute(value, axis, [(source, source + steps) for source in range(l...  116 us
    dot_general x19, matrix products, couple(): jnp.einsum('bjki,bk->bji', coupling, vector, precision=HIGHEST_PRECISION)  113 us
    psum x1, waiting for transfers between devices, broadcast(): return lax.psum(jnp.where(mine, shard, jnp.zeros_like(shard)), axis)  69.6 us
    select_n x8, other arithmetic, hop(): return jax.tree.map(lambda a, b: jnp.where(reached, a, b), new, before)  24.5 us
  transfers between devices with their start and end apart: 41, of which 3 were waited for; matrix products, arithmetic and copies ran while one was open for 26% of the time, Pallas kernels for 0%

commit v1 on v0

v1 whole, which is shorter than its diff:
```python
import jax
import jax.numpy as jnp
from jax import lax
from jax.sharding import PartitionSpec as P

FINE = 2
SUB = 2
CG_ITERS = 8


def passed_along(value, axis, steps):
    count = lax.axis_size(axis)
    leading, last = (max(0, -steps), min(count, count - steps))
    return lax.ppermute(value, axis, [(source, source + steps) for source in range(leading, last)])


def shifted(value, axis, steps):
    count = lax.axis_size(axis)
    return lax.ppermute(value, axis, [(source, (source + steps) % count) for source in range(count)])


def exchange(partials, axis, down=None, up=None):
    count = lax.axis_size(axis)
    mine = lax.axis_index(axis)
    width = partials.shape[0]
    row = jnp.zeros((1, 128), jnp.float32).at[0, :width].set(partials)
    received = [row]
    got_down = None
    got_up = None
    for steps in range(1, count):
        pieces = [row]
        if steps == 1 and down is not None:
            pieces.append(down)
        if steps == count - 1 and up is not None:
            pieces.append(up)
        payload = jnp.concatenate(pieces, axis=0) if len(pieces) > 1 else row
        arrived = shifted(payload, axis, steps)
        received.append(arrived[:1])
        offset = 1
        if steps == 1 and down is not None:
            got_down = arrived[offset : offset + down.shape[0]]
            offset += down.shape[0]
        if steps == count - 1 and up is not None:
            got_up = arrived[offset : offset + up.shape[0]]
    stacked = jnp.concatenate(received, axis=0)[:, :width]
    order = (mine - jnp.arange(count)) % count
    by_source = jnp.take(stacked, order, axis=0)
    total = by_source[0]
    for source in range(1, count):
        total = total + by_source[source]
    if got_down is not None:
        got_down = jnp.where(mine == 0, jnp.zeros_like(got_down), got_down)
    if got_up is not None:
        got_up = jnp.where(mine == count - 1, jnp.zeros_like(got_up), got_up)
    return total, got_down, got_up


def ionic_update(voltage, gating, conductance, gate_center, gate_slope, gate_rate, reversal):
    for substep in range(SUB):
        steady = jax.nn.sigmoid((voltage[None, :] - gate_center) / gate_slope)
        damping = jnp.exp(-gate_rate * (0.5 + steady))
        gating = steady + (gating - steady) * damping
        current = jnp.sum(conductance * gating * (voltage[None, :] - reversal), axis=0)
        voltage = voltage - current
    return (voltage, gating)


def body(
    states_old,
    coupling,
    gate_center,
    gate_slope,
    gate_rate,
    reversal,
    conductance,
    stimulus,
    coarse_rate,
):
    num_blocks = coupling.shape[0]
    tile_width = coupling.shape[2]
    zero_rows = jnp.zeros((2, tile_width), jnp.float32)

    def couple_local(vector, upper_rows):
        extended = jnp.concatenate([vector, upper_rows], axis=0)
        ahead_sum = jnp.sum(
            coupling[:, 0] * extended[1 : num_blocks + 1, None, :]
            + coupling[:, 1] * extended[2 : num_blocks + 2, None, :],
            axis=-1,
        )
        carried = jnp.sum(coupling * vector[:, None, :, None], axis=2)
        inner = jnp.concatenate([zero_rows[:1], carried[:-1, 0]], axis=0) + jnp.concatenate(
            [zero_rows, carried[:-2, 1]], axis=0
        )
        spilled = jnp.stack([carried[-1, 0] + carried[-2, 1], carried[-1, 1]])
        return ahead_sum + inner, spilled

    def pad_head(rows):
        return jnp.concatenate(
            [rows, jnp.zeros((num_blocks - 2, tile_width), jnp.float32)], axis=0
        )

    ones = jnp.ones((num_blocks, tile_width), jnp.float32)
    local_degree, spilled = couple_local(ones, passed_along(ones[:2], "space", -1))
    degree = local_degree + pad_head(passed_along(spilled, "space", 1))

    voltage = states_old[0, 0]
    gating = states_old[0, 1:]
    for fine_step in range(FINE):
        voltage, gating = ionic_update(
            voltage, gating, conductance, gate_center, gate_slope, gate_rate, reversal
        )
        voltage = voltage + stimulus[0]
        right_side = voltage.reshape(num_blocks, tile_width)
        iterate = right_side
        upper = passed_along(right_side[:2], "space", -1)
        partial, spilled = couple_local(right_side, upper)
        arrived = passed_along(spilled, "space", 1)
        mapped = right_side + degree * right_side - partial - pad_head(arrived)
        residual = right_side - mapped
        norm_now, _, residual_up = exchange(
            jnp.sum(residual * residual)[None], "space", up=residual[:2]
        )
        norm_now = norm_now[0]
        direction = residual
        direction_up = residual_up
        for iteration in range(CG_ITERS):
            partial, spilled = couple_local(direction, direction_up)
            local_mapped = direction + degree * direction - partial
            curvature_part = jnp.sum(direction * local_mapped) - jnp.sum(direction_up * spilled)
            curvature, arrived, _ = exchange(curvature_part[None], "space", down=spilled)
            mapped = local_mapped - pad_head(arrived)
            step_size = norm_now / curvature[0]
            iterate = iterate + step_size * direction
            residual = residual - step_size * mapped
            norm_next, _, residual_up = exchange(
                jnp.sum(residual * residual)[None], "space", up=residual[:2]
            )
            norm_next = norm_next[0]
            direction = residual + norm_next / norm_now * direction
            direction_up = residual_up + norm_next / norm_now * direction_up
            norm_now = norm_next
        voltage = iterate.reshape(-1)
    fine_state = jnp.concatenate([voltage[None, :], gating], axis=0)
    exponent = 1.0 + jax.nn.sigmoid(states_old[0, 0])
    factor = jnp.exp(-coarse_rate * exponent[None, :])
    offset = fine_state - factor * states_old[0]

    slices = lax.axis_size("tm")
    assert slices & (slices - 1) == 0
    packed = shifted(jnp.concatenate([exponent[None, :], offset], axis=0), "tm", 1)
    span = 1
    while span < slices:
        earlier = shifted(packed, "tm", span)
        decay = jnp.exp(-coarse_rate * packed[0][None, :])
        packed = jnp.concatenate(
            [(packed[0] + earlier[0])[None, :], decay * earlier[1:] + packed[1:]], axis=0
        )
        span *= 2
    loop_a = jnp.exp(-coarse_rate * packed[0][None, :])
    new_state = packed[1:] / (1.0 - loop_a)
    return (new_state[None], new_state[0][None])


def solution(mesh):
    return jax.shard_map(
        body,
        mesh=mesh,
        in_specs=(
            P("tm", None, "space"),
            P("space", None, None, None),
            P(),
            P(),
            P(),
            P(),
            P(None, "space"),
            P("tm", "space"),
            P(None, "space"),
        ),
        out_specs=(P("tm", None, "space"), P("tm", "space")),
        check_vma=False,
    )
```

time: 1180 us -> 767 us (0.65)
  matrix products: 412 us -> 0 us
  blocking collectives: 300 us -> 0 us
  other arithmetic: 63.3 us -> 202 us
  between operations: 54.8 us -> 136 us
  local copies, waits for them, and re-layouts: 5.95 us -> 54.6 us
  waiting for transfers between devices: 215 us -> 237 us
  starting transfers between devices: 116 us -> 128 us
    dot_general x57 -> x0, matrix products: 412 us -> none  [the longest x38 299 us: matvec_rows(): return jnp.einsum('bik,bk->bi', tiles, values, precision=HIGHEST_PRECISION)]
    psum x30 -> x0, blocking collectives: 300 us -> none  [the longest x16 161 us: squares(): return lax.psum(jnp.sum(vector * vector), 'space')]
    ppermute x0 -> x100, waiting for transfers between devices: none -> 237 us  [shifted(): lax.ppermute(value, axis, [(source, (source + steps) % count) for source...]
    reduce_sum x30 -> x84, other arithmetic: 19.3 us -> 186 us  [the longest x18 81.5 us: couple_local(): jnp.sum(coupling[:, 0] * extended[1:num_blocks + 1, None, :] + coupling[:...]
    all_gather x2 -> x0, waiting for transfers between devices: 145 us -> none  [entering(): everything = jax.tree.map(lambda part: lax.all_gather(part, axis), shard)]
    ppermute x0 -> x100, starting transfers between devices: none -> 109 us  [shifted(): lax.ppermute(value, axis, [(source, (source + steps) % count) for source...]
    ppermute x38 -> x6, starting transfers between devices: 116 us -> 18.7 us  [passed_along(): lax.ppermute(value, axis, [(source, source + steps) for source in range(l...]
    psum x1 -> x0, waiting for transfers between devices: 69.6 us -> none  [broadcast(): return lax.psum(jnp.where(mine, shard, jnp.zeros_like(shard)), axis)]
  transfers between devices with their start and end apart: 41 -> 106, of which waited for: 3 -> 79; matrix products, arithmetic and copies ran while one was open for 26% -> 5% of each run, Pallas kernels for 0% -> 0%
where the time goes in v1:
time: 767 us; the launch traced here: 757 us
  waiting for transfers between devices  237 us (31%)
  other arithmetic  202 us (26%)
  between operations  136 us (18%)
  starting transfers between devices  128 us (17%)
  local copies, waits for them, and re-layouts  54.6 us (7%)
    ppermute x100, waiting for transfers between devices, shifted(): lax.ppermute(value, axis, [(source, (source + steps) % count) for source...  237 us
    ppermute x100, starting transfers between devices, shifted(): lax.ppermute(value, axis, [(source, (source + steps) % count) for source...  109 us
    reduce_sum x18, other arithmetic, couple_local(): jnp.sum(coupling[:, 0] * extended[1:num_blocks + 1, None, :] + coupling[:...  81.5 us
    reduce_sum x18, other arithmetic, couple_local(): carried = jnp.sum(coupling * vector[:, None, :, None], axis=2)  74.4 us
    gather x32, local copies, waits for them, and re-layouts, exchange(): by_source = jnp.take(stacked, order, axis=0)  23.4 us
    slice x32, local copies, waits for them, and re-layouts, exchange(): total = total + by_source[source]  21 us
    ppermute x6, starting transfers between devices, passed_along(): lax.ppermute(value, axis, [(source, source + steps) for source in range(l...  18.7 us
  transfers between devices with their start and end apart: 106, of which 79 were waited for; matrix products, arithmetic and copies ran while one was open for 5% of the time, Pallas kernels for 0%

profile of v1, /device:TPU:0, one launch (start us, length us, event | category | flops | bytes accessed | tf_op | source)
XLA Modules:
  0.0 757.2 jit_solution(16242360311304413307)
XLA Ops:
  12.9 6.2 collective-permute-start.1
  24.1 5.7 fusion.3
  43.4 4.7 fusion.5
  84.1 4.7 fusion.7
  121.1 4.7 fusion.9
  158.3 4.7 fusion.11
  195.3 4.7 fusion.13
  232.7 4.7 fusion.15
  269.5 4.7 fusion.17
  307.0 4.7 fusion.19
  329.8 4.4 multiply_reduce_fusion.8
  335.6 4.5 collective-permute-start.53
  355.1 4.6 fusion.23
  395.7 4.6 fusion.25
  433.1 4.6 fusion.27
  470.1 4.6 fusion.29
  507.0 4.6 fusion.31
  543.9 4.6 fusion.33
  581.5 4.6 fusion.35
  618.6 4.8 fusion.37
  641.0 20.7 %collective-permute-done.102 = f32[42,8192]{1,0:T(8,128)S(1)} collective-permute-done((f32[42,8192]{1,0:T(8,128)S(1)}, f32[42,8192]{1,0:T(8,128)S(1)}, u32[]{:S(2)}, u32[]{:S(2)}) %collective-permute-start.102) | collective-permute-done | bytes 1376288 | tf_op jit(solution)/shard_map/ppermute | solution.py:19
  661.8 20.7 %collective-permute-done.103 = f32[42,8192]{1,0:T(8,128)S(1)} collective-permute-done((f32[42,8192]{1,0:T(8,128)S(1)}, f32[42,8192]{1,0:T(8,128)S(1)}, u32[]{:S(2)}, u32[]{:S(2)}) %collective-permute-start.103) | collective-permute-done | bytes 1376288 | tf_op jit(solution)/shard_map/ppermute | solution.py:19
  683.4 34.5 %collective-permute-done.104 = f32[42,8192]{1,0:T(8,128)S(1)} collective-permute-done((f32[42,8192]{1,0:T(8,128)S(1)}, f32[42,8192]{1,0:T(8,128)S(1)}, u32[]{:S(2)}, u32[]{:S(2)}) %collective-permute-start.104) | collective-permute-done | bytes 1376288 | tf_op jit(solution)/shard_map/ppermute | solution.py:19
  720.2 32.6 %collective-permute-done.105 = f32[42,8192]{1,0:T(8,128)S(1)} collective-permute-done((f32[42,8192]{1,0:T(8,128)S(1)}, f32[42,8192]{1,0:T(8,128)S(1)}, u32[]{:S(2)}, u32[]{:S(2)}) %collective-permute-start.105) | collective-permute-done | bytes 1376288 | tf_op jit(solution)/shard_map/ppermute | solution.py:19
  (742 shorter events, 417.5 us)
Async XLA Ops:
  0.7 23.3 %collective-permute-start = (f32[2,128]{1,0:T(2,128)S(1)}, f32[2,128]{1,0:T(2,128)S(1)}, u32[]{:S(2)}, u32[]{:S(2)}) collective-permute-start(f32[2,128]{1,0:T(2,128)S(1)} %slice.1718), channel_id=1, source_target_pairs={{1,0},{2,1},{3,2},{5,4},{6,5},{7,6},{9,8},{10,9},{11,10},{13,12},{... | collective-permute-start | bytes 3080 | tf_op jit(solution)/shard_map/ppermute | solution.py:14
  9.5 14.5 %collective-permute-start.2 = (f32[2,128]{1,0:T(2,128)S(1)}, f32[2,128]{1,0:T(2,128)S(1)}, u32[]{:S(2)}, u32[]{:S(2)}) collective-permute-start(f32[2,128]{1,0:T(2,128)S(1)} %slice.2171), channel_id=1, source_target_pairs={{1,0},{2,1},{3,2},{5,4},{6,5},{7,6},{9,8},{10,9},{11,10},{13,12},{... | collective-permute-start | bytes 3080 | tf_op jit(solution)/shard_map/ppermute | solution.py:14
  12.9 16.9 %collective-permute-start.1 = (f32[2,128]{1,0:T(2,128)S(1)}, f32[2,128]{1,0:T(2,128)S(1)}, u32[]{:S(2)}, u32[]{:S(2)}) collective-permute-start(f32[2,128]{1,0:T(2,128)S(1)} %pad_maximum_fusion.85), channel_id=1, source_target_pairs={{0,1},{1,2},{2,3},{4,5},{5,6},{6,7},{8,9},{9,10},{10,11},{12,13},{... | collective-permute-start | bytes 3080 | tf_op jit(solution)/shard_map/ppermute | solution.py:14
  19.1 10.7 %collective-permute-start.3 = (f32[2,128]{1,0:T(2,128)S(1)}, f32[2,128]{1,0:T(2,128)S(1)}, u32[]{:S(2)}, u32[]{:S(2)}) collective-permute-start(f32[2,128]{1,0:T(2,128)S(1)} %pad_maximum_fusion.86), channel_id=1, source_target_pairs={{0,1},{1,2},{2,3},{4,5},{5,6},{6,7},{8,9},{9,10},{10,11},{12,13},{... | collective-permute-start | bytes 3080 | tf_op jit(solution)/shard_map/ppermute | solution.py:14
  31.8 22.9 %collective-permute-start.5 = (f32[1,128]{1,0:T(1,128)S(1)}, f32[1,128]{1,0:T(1,128)S(1)}, u32[]{:S(2)}, u32[]{:S(2)}) collective-permute-start(f32[1,128]{1,0:T(1,128)S(1)} %scatter.106), channel_id=1, source_target_pairs={{0,2},{1,3},{2,0},{3,1},{4,6},{5,7},{6,4},{7,5},{8,10},{9,11},{10,... | collective-permute-start | bytes 1544 | tf_op jit(solution)/shard_map/ppermute | solution.py:19
  33.3 21.4 %collective-permute-start.4 = (f32[1,128]{1,0:T(1,128)S(1)}, f32[1,128]{1,0:T(1,128)S(1)}, u32[]{:S(2)}, u32[]{:S(2)}) collective-permute-start(f32[1,128]{1,0:T(1,128)S(1)} %scatter.106), channel_id=1, source_target_pairs={{0,1},{1,2},{2,3},{3,0},{4,5},{5,6},{6,7},{7,4},{8,9},{9,10},{10,1... | collective-permute-start | bytes 1544 | tf_op jit(solution)/shard_map/ppermute | solution.py:19
  50.6 10.4 %collective-permute-start.9 = (f32[1,128]{1,0:T(1,128)S(1)}, f32[1,128]{1,0:T(1,128)S(1)}, u32[]{:S(2)}, u32[]{:S(2)}) collective-permute-start(f32[1,128]{1,0:T(1,128)S(1)} %scatter.109), channel_id=1, source_target_pairs={{0,3},{1,0},{2,1},{3,2},{4,7},{5,4},{6,5},{7,6},{8,11},{9,8},{10,9... | collective-permute-start | bytes 1544 | tf_op jit(solution)/shard_map/ppermute | solution.py:19
  54.8 6.3 collective-permute-start.8
  69.6 5.5 collective-permute-start.10
  91.3 5.4 collective-permute-start.13
  128.4 5.4 collective-permute-start.19
  202.6 5.4 collective-permute-start.31
  334.2 6.0 collective-permute-start.52
  335.6 5.9 collective-permute-start.53
  343.3 23.1 %collective-permute-start.55 = (f32[1,128]{1,0:T(1,128)S(1)}, f32[1,128]{1,0:T(1,128)S(1)}, u32[]{:S(2)}, u32[]{:S(2)}) collective-permute-start(f32[1,128]{1,0:T(1,128)S(1)} %scatter.134), channel_id=1, source_target_pairs={{0,2},{1,3},{2,0},{3,1},{4,6},{5,7},{6,4},{7,5},{8,10},{9,11},{10,... | collective-permute-start | bytes 1544 | tf_op jit(solution)/shard_map/ppermute | solution.py:19
  345.1 21.4 %collective-permute-start.54 = (f32[1,128]{1,0:T(1,128)S(1)}, f32[1,128]{1,0:T(1,128)S(1)}, u32[]{:S(2)}, u32[]{:S(2)}) collective-permute-start(f32[1,128]{1,0:T(1,128)S(1)} %scatter.134), channel_id=1, source_target_pairs={{0,1},{1,2},{2,3},{3,0},{4,5},{5,6},{6,7},{7,4},{8,9},{9,10},{10,1... | collective-permute-start | bytes 1544 | tf_op jit(solution)/shard_map/ppermute | solution.py:19
  362.3 10.4 %collective-permute-start.59 = (f32[1,128]{1,0:T(1,128)S(1)}, f32[1,128]{1,0:T(1,128)S(1)}, u32[]{:S(2)}, u32[]{:S(2)}) collective-permute-start(f32[1,128]{1,0:T(1,128)S(1)} %scatter.135), channel_id=1, source_target_pairs={{0,3},{1,0},{2,1},{3,2},{4,7},{5,4},{6,5},{7,6},{8,11},{9,8},{10,9... | collective-permute-start | bytes 1544 | tf_op jit(solution)/shard_map/ppermute | solution.py:19
  366.4 6.3 collective-permute-start.58
  403.0 5.4 collective-permute-start.63
  418.5 5.5 collective-permute-start.66
  641.0 20.8 %collective-permute-start.102 = (f32[42,8192]{1,0:T(8,128)S(1)}, f32[42,8192]{1,0:T(8,128)S(1)}, u32[]{:S(2)}, u32[]{:S(2)}) collective-permute-start(f32[42,8192]{1,0:T(8,128)S(1)} %pad_maximum_fusion), channel_id=1, source_target_pairs={{0,4},{4,8},{8,12},{12,16},{16,20},{20,24},{24,28},{28,0},{1,5},{5... | collective-permute-start | bytes 4128776 | tf_op jit(solution)/shard_map/ppermute | solution.py:19
  661.8 20.7 %collective-permute-start.103 = (f32[42,8192]{1,0:T(8,128)S(1)}, f32[42,8192]{1,0:T(8,128)S(1)}, u32[]{:S(2)}, u32[]{:S(2)}) collective-permute-start(f32[42,8192]{1,0:T(8,128)S(1)} %collective-permute-done.102), channel_id=1, source_target_pairs={{0,4},{4,8},{8,12},{12,16},{16,20},{20,24},{24,28},{28,0},{1,5},{5... | collective-permute-start | bytes 4128776 | tf_op jit(solution)/shard_map/ppermute | solution.py:19
  683.3 34.6 %collective-permute-start.104 = (f32[42,8192]{1,0:T(8,128)S(1)}, f32[42,8192]{1,0:T(8,128)S(1)}, u32[]{:S(2)}, u32[]{:S(2)}) collective-permute-start(f32[42,8192]{1,0:T(8,128)S(1)} %pad_maximum_fusion.1), channel_id=1, source_target_pairs={{0,8},{4,12},{8,16},{12,20},{16,24},{20,28},{24,0},{28,4},{1,9},{5... | collective-permute-start | bytes 4128776 | tf_op jit(solution)/shard_map/ppermute | solution.py:19
  718.6 34.2 %collective-permute-start.105 = (f32[42,8192]{1,0:T(8,128)S(1)}, f32[42,8192]{1,0:T(8,128)S(1)}, u32[]{:S(2)}, u32[]{:S(2)}) collective-permute-start(f32[42,8192]{1,0:T(8,128)S(1)} %pad_maximum_fusion.2), channel_id=1, source_target_pairs={{0,16},{4,20},{8,24},{12,28},{16,0},{20,4},{24,8},{28,12},{1,17},{... | collective-permute-start | bytes 4128776 | tf_op jit(solution)/shard_map/ppermute | solution.py:19
  (94 other events, 562.1 us)
